TPU v7x, 32 devices: a whole 2x2x4 slice. The times are simulated.
32 devices in a mesh: shift: 2 (over y), space: 4 (over z), orb: 2 (over x), grid: 2 (over core).
Axes of the slice: x: 2, y: 2, z: 4, core: 2. Of those that a mesh axis runs over, the one named last changes fastest.
Arguments:
- support: bfloat16 [128, 9, 15, 256], P(('shift', 'space', 'orb'), None, None, 'grid'), parts along dimension 0, may hold values from -0.75 to 0.75
- anchor: int32 [128], P(('shift', 'space', 'orb')), parts along dimension 0, may hold values from 0 to 63, as said below
- kernel: float32 [512, 9, 9], P(('shift', 'space', 'orb')), parts along dimension 0, may hold values from -2.1 to 2.1
- pair_owner: int32 [512], P(('shift', 'space', 'orb')), parts along dimension 0, may hold values from 0 to 63, as said below
- pair_partner: int32 [512], P(('shift', 'space', 'orb')), parts along dimension 0, may hold values from 0 to 63, as said below
- pair_live: int32 [512], P(('shift', 'space', 'orb')), parts along dimension 0, may hold values 0 or 1
- v_ext: float32 [128, 256], P(('shift', 'space'), 'grid'), parts along dimension 0, may hold values from -6 to 6
Outputs:
- density: float32 [128, 256], P(('shift', 'space'), 'grid'), parts along dimension 0
- hamiltonian: float32 [512, 9, 9], P(('shift', 'space', 'orb')), parts along dimension 0
There are 2 independent parts, one for each index of `shift`. A program takes and returns all parts, laid end to end along the dimension named above; each array names one. Nothing has to cross between parts.
Inputs may be any that keep to these rules, and one draw needn't show every extreme that they name: Atom a lies in spatial domain a // 16, and its box starts at a plane of that domain: anchor[a] // 16 = a // 16. The owner of slot p is one of the 8 atoms of block p // 32: pair_owner[p] // 8 = p // 32. `pair_partner`: the partner of a slot lies in its owner's spatial domain or in one of the two adjacent domains, counted periodically, and its box shares at least one plane with the owner's box: |gap| <= 14.
All inputs are finite; a program needn't handle non-finite values. No bound on the sum of `pair_live` on one device may be relied on, other than what follows from the above.
Results may differ from a plain program's by a relative error of at most 0.0028.
Values may be sent and summed in bfloat16 or wider, within the bound.
A program may use at most 64 MiB of HBM per device.

v0:
```python
import jax
import jax.numpy as jnp
from jax import lax
from jax.sharding import PartitionSpec as P


def shifted(value, axis, steps):
    count = lax.axis_size(axis)
    pairs = [(source, (source + steps) % count) for source in range(count)]
    return lax.ppermute(value, axis, pairs)


def shift_planes(rows, plane_gap, box_depth):
    index = jnp.arange(box_depth, dtype=jnp.int32)[None, :] + plane_gap[:, None]
    inside = (index >= 0) & (index < box_depth)
    picked = jnp.take_along_axis(rows, jnp.clip(index, 0, box_depth - 1)[:, None, :, None], axis=2)
    return jnp.where(inside[:, None, :, None], picked, jnp.zeros_like(picked))


def respond(field):
    return field / jnp.sqrt(1.0 + field * field)


def on_device(support, anchor, kernel, pair_owner, pair_partner, pair_live, v_ext):
    per_device, functions, box_depth, points = support.shape
    pair_count = kernel.shape[0]
    slab_rows = v_ext.shape[0]
    orb_count = lax.axis_size("orb")
    space_count = lax.axis_size("space")
    per_domain = per_device * orb_count
    total_planes = slab_rows * space_count
    domain = lax.axis_index("space")
    orb_index = lax.axis_index("orb")
    own_block = domain * orb_count + orb_index
    below_support, below_anchor = shifted((support, anchor), "space", 1)
    above_support, above_anchor = shifted((support, anchor), "space", -1)
    lower_support, domain_support, upper_support, lower_anchor, domain_anchor, upper_anchor = (
        lax.all_gather(below_support, "orb", axis=0, tiled=True),
        lax.all_gather(support, "orb", axis=0, tiled=True),
        lax.all_gather(above_support, "orb", axis=0, tiled=True),
        lax.all_gather(below_anchor, "orb", axis=0, tiled=True),
        lax.all_gather(anchor, "orb", axis=0, tiled=True),
        lax.all_gather(above_anchor, "orb", axis=0, tiled=True),
    )
    window_support = jnp.concatenate([lower_support, domain_support, upper_support], axis=0)
    window_anchor = jnp.concatenate([lower_anchor, domain_anchor, upper_anchor], axis=0)
    partner_domain = pair_partner // per_domain
    relative = (partner_domain - domain + 1 + space_count) % space_count
    window_index = relative * per_domain + pair_partner % per_domain
    owner_local = pair_owner - own_block * per_device
    plane_gap = (
        (anchor[owner_local] - window_anchor[window_index] + total_planes // 2) % total_planes
        - total_planes // 2
    ).astype(jnp.int32)
    alive = pair_live.astype(jnp.float32)
    block_count = pair_count // pair_count
    index_blocks = window_index.reshape(block_count, pair_count)
    gap_blocks = plane_gap.reshape(block_count, pair_count)
    owner_blocks = owner_local.reshape(block_count, pair_count)
    kernel_blocks = (kernel * alive[:, None, None]).reshape(
        block_count, pair_count, functions, functions
    )
    atom_ids = jnp.arange(per_device, dtype=jnp.int32)

    def aux_step(total, items):
        rows_index, gaps, kern, owners = items
        moved = shift_planes(window_support[rows_index], gaps, box_depth)
        terms = jnp.einsum(
            "pst,ptjq->psjq", kern, moved.astype(jnp.float32), precision=lax.Precision.HIGHEST
        )
        table = (owners[None, :] == atom_ids[:, None]).astype(jnp.float32)
        return (
            total + jnp.einsum("ap,psjq->asjq", table, terms, precision=lax.Precision.HIGHEST),
            None,
        )

    start_aux = jnp.zeros((per_device, functions, box_depth, points), jnp.float32)
    aux, _ = lax.scan(aux_step, start_aux, (index_blocks, gap_blocks, kernel_blocks, owner_blocks))
    deposit_terms = jnp.sum(support.astype(jnp.float32) * aux, axis=1)
    offset = anchor - domain * slab_rows
    local_plane = offset[:, None] + jnp.arange(box_depth, dtype=jnp.int32)[None, :]
    placing = (
        jnp.arange(2 * slab_rows, dtype=jnp.int32)[:, None, None] == local_plane[None, :, :]
    ).astype(jnp.float32)
    deposit = jnp.einsum("zaj,ajq->zq", placing, deposit_terms, precision=lax.Precision.HIGHEST)
    summed = lax.psum(deposit, "orb")
    incoming = shifted(summed[slab_rows:], "space", 1)
    density = summed[:slab_rows] + incoming
    potential = v_ext + respond(density)
    next_potential = shifted(potential, "space", -1)
    both_slabs = jnp.concatenate([potential, next_potential], axis=0)
    box_potential = jnp.einsum("zaj,zq->ajq", placing, both_slabs, precision=lax.Precision.HIGHEST)
    weighted = (support.astype(jnp.float32) * box_potential[:, None, :, :]).astype(jnp.bfloat16)

    def ham_block(items):
        rows_index, gaps, owners = items
        moved = shift_planes(window_support[rows_index], gaps, box_depth)
        owner_rows = weighted[owners]
        return jnp.einsum("psjq,ptjq->pst", owner_rows, moved, preferred_element_type=jnp.float32)

    partial_blocks = lax.map(ham_block, (index_blocks, gap_blocks, owner_blocks)).reshape(
        pair_count, functions, functions
    )
    hamiltonian = lax.psum(partial_blocks, "grid") * alive[:, None, None]
    return (density, hamiltonian)


def solution(mesh):
    placed = (
        P(("shift", "space", "orb"), None, None, "grid"),
        P(("shift", "space", "orb")),
        P(("shift", "space", "orb"), None, None),
        P(("shift", "space", "orb")),
        P(("shift", "space", "orb")),
        P(("shift", "space", "orb")),
        P(("shift", "space"), "grid"),
    )
    return jax.shard_map(
        on_device,
        mesh=mesh,
        in_specs=placed,
        out_specs=(P(("shift", "space"), "grid"), P(("shift", "space", "orb"), None, None)),
        check_vma=False,
    )
```

profile of v0, /device:TPU:0, one launch (start us, length us, event | category | flops | bytes accessed | tf_op | source)
XLA Modules:
  0.0 81.6 jit_solution(5677399734707426305)
XLA Ops:
  0.7 3.1 %collective-permute-start = (s32[8]{0:T(128)}, s32[8]{0:T(128)S(1)}, u32[]{:S(2)}, u32[]{:S(2)}) collective-permute-start(s32[8]{0:T(128)} %param.10), channel_id=1, source_target_pairs={{0,4},{4,8},{8,12},{12,0},{1,5},{5,9},{9,13},{13,1},{2,6},{6,10},{... | collective-permute-start | bytes 104 | tf_op jit(solution)/shard_map/ppermute | solution.py:10
  3.8 2.1 %collective-permute-start.1 = (s32[8]{0:T(128)}, s32[8]{0:T(128)S(1)}, u32[]{:S(2)}, u32[]{:S(2)}) collective-permute-start(s32[8]{0:T(128)} %param.10), channel_id=1, source_target_pairs={{0,12},{4,0},{8,4},{12,8},{1,13},{5,1},{9,5},{13,9},{2,14},{6,2},{... | collective-permute-start | bytes 104 | tf_op jit(solution)/shard_map/ppermute | solution.py:10
  5.9 3.8 %collective-permute-start.3 = (bf16[8,9,15,128]{3,0,2,1:T(8,128)(2,1)}, bf16[8,9,15,128]{3,0,2,1:T(8,128)(2,1)S(1)}, u32[]{:S(2)}, u32[]{:S(2)}) collective-permute-start(bf16[8,9,15,128]{3,0,2,1:T(8,128)(2,1)} %param.9), channel_id=1, source_target_pairs={{0,12},{4,0},{8,4},{12,8},{1,13},{5,1},{9,5},{13,9},{2,14},{6,2},{... | collective-permute-start | bytes 829448 | tf_op jit(solution)/shard_map/ppermute | solution.py:10
  9.7 8.4 %all_gather.22 = bf16[16,9,15,128]{3,0,2,1:T(8,128)(2,1)S(1)} all-gather(bf16[8,9,15,128]{3,0,2,1:T(8,128)(2,1)} %param.9), channel_id=1, replica_groups=mesh['shift'=2,'space'=4,'orb'=2,'grid'=2] {'orb'}, dimensions={0}, use_global_device_ids=true | all-gather | bytes 829440 | tf_op jit(solution)/shard_map/all_gather | solution.py:39
  18.1 0.7 compare_select_fusion.1
  18.8 0.7 compare_select_fusion.2
  19.5 1.4 %gather_fusion = s32[32]{0:T(128)S(1)} fusion(s32[8]{0:T(128)} %param.10, s32[1024]{0:T(1024)S(1)} %pad_clamp_fusion.1), kind=kCustom, calls=%fused_computation.1 | custom fusion | bytes 384 | tf_op jit(solution)/shard_map/gather | solution.py:52
  23.3 4.3 %all-reduce.3 = (s32[16]{0:T(128)S(1)}, s32[16]{0:T(128)S(1)}, s32[16]{0:T(128)S(1)}) all-reduce(s32[16]{0:T(128)S(1)} %dynamic-update-slice.2, s32[16]{0:T(128)S(1)} %dynamic-update-slice.1, s32[16]{0:T(128)S(1)} %dynamic-update-slice), channel_id=1, replica_groups=mesh['shift'=2,'space'=4,'orb'=2,'grid'=2] {'orb'}, use_global_device_ids=true, to_apply=%add.2 | all-reduce | flops 48 | bytes 384
  27.6 0.7 gather_fusion.1
  28.7 8.0 %all_gather.21 = bf16[16,9,15,128]{3,0,2,1:T(8,128)(2,1)S(1)} all-gather(bf16[8,9,15,128]{3,0,2,1:T(8,128)(2,1)S(1)} %collective-permute-done.2), channel_id=1, replica_groups=mesh['shift'=2,'space'=4,'orb'=2,'grid'=2] {'orb'}, dimensions={0}, use_global_device_ids=true | all-gather | bytes 829440 | tf_op jit(solution)/shard_map/all_gather | solution.py:38
  36.8 7.2 %all_gather.23 = bf16[16,9,15,128]{3,0,2,1:T(8,128)(2,1)S(1)} all-gather(bf16[8,9,15,128]{3,0,2,1:T(8,128)(2,1)S(1)} %collective-permute-done.3), channel_id=1, replica_groups=mesh['shift'=2,'space'=4,'orb'=2,'grid'=2] {'orb'}, dimensions={0}, use_global_device_ids=true | all-gather | bytes 829440 | tf_op jit(solution)/shard_map/all_gather | solution.py:40
  44.5 0.8 gather_fusion.2
  45.3 1.8 %copy.40 = bf16[32,9,15,128]{3,1,2,0:T(8,128)(2,1)} copy(bf16[32,9,15,128]{3,2,1,0:T(8,128)(2,1)S(1)} %gather_fusion.2) | data formatting | bytes 2211840 | tf_op jit(solution)/shard_map/while/body/eval_jaxpr/gather | solution.py:67
  47.1 5.2 %gather_fusion.4 = bf16[480,9,128]{2,1,0:T(8,128)(2,1)S(1)} fusion(bf16[32,9,15,128]{3,1,2,0:T(8,128)(2,1)} %copy.40, s32[480]{0:T(512)S(1)} %reshape.174), kind=kCustom, calls=%fused_computation.clone | custom fusion | bytes 2215680 | tf_op jit(solution)/shard_map/while/body/eval_jaxpr/jit(take_along_axis)/gather | solution.py:16
  52.7 2.1 %fusion.4 = f32[32,9,15,128]{3,1,2,0:T(8,128)S(1)} fusion(bf16[32,9,15,128]{3,2,0,1:T(8,128)(2,1)S(1)} %bitcast_select_fusion, f32[32,9,9]{2,1,0:T(8,128)S(1)} %copy.36, f32[32]{0:T(128)S(1)} %convert_element_type.16), kind=kOutput, calls=%fused_computation.9 | convolution fusion | flops 59722272 | bytes 3328256 | tf_op jit(solution)/shard_map/while/body/eval_jaxpr/pst,ptjq->psjq/dot_general | solution.py:68
  54.8 1.5 %fusion.10 = f32[8,15,128]{2,0,1:T(8,128)S(1)} fusion(f32[32,9,15,128]{3,1,2,0:T(8,128)S(1)} %fusion.4, bf16[8,9,15,128]{3,0,2,1:T(8,128)(2,1)S(1)} %copy-done.1, s32[32]{0:T(128)S(1)} %get-tuple-element.62), kind=kOutput, calls=%fused_computation.14 | convolution fusion | flops 53483776 | bytes 2549888 | tf_op jit(solution)/shard_map/while/body/eval_jaxpr/ap,psjq->asjq/dot_general | solution.py:73
  56.6 8.3 %psum.14 = f32[32,128]{1,0:T(8,128)S(1)} all-reduce(f32[32,128]{1,0:T(8,128)S(1)} %convolution_bitcast_fusion), channel_id=1, replica_groups=mesh['shift'=2,'space'=4,'orb'=2,'grid'=2] {'orb'}, use_global_device_ids=true, to_apply=%region_1.3 | all-reduce | flops 4096 | bytes 32768 | tf_op jit(solution)/shard_map/psum | solution.py:86
  64.9 5.4 %collective-permute-done.4 = f32[16,128]{1,0:T(8,128)S(1)} collective-permute-done((f32[16,128]{1,0:T(8,128)S(1)}, f32[16,128]{1,0:T(8,128)S(1)}, u32[]{:S(2)}, u32[]{:S(2)}) %collective-permute-start.4) | collective-permute-done | bytes 8224 | tf_op jit(solution)/shard_map/ppermute | solution.py:10
  70.4 0.6 multiply_add_fusion
  71.1 3.6 %collective-permute-done.5 = f32[16,128]{1,0:T(8,128)S(1)} collective-permute-done((f32[16,128]{1,0:T(8,128)S(1)}, f32[16,128]{1,0:T(8,128)S(1)}, u32[]{:S(2)}, u32[]{:S(2)}) %collective-permute-start.5) | collective-permute-done | bytes 8224 | tf_op jit(solution)/shard_map/ppermute | solution.py:10
  74.9 0.8 gather_fusion.3
  75.7 1.0 %fusion.13 = f32[32,9,9]{2,1,0:T(8,128)S(1)} fusion(bf16[32,9,15,128]{3,2,0,1:T(8,128)(2,1)S(1)} %bitcast_select_fusion, bf16[32,9,15,128]{3,2,1,0:T(8,128)(2,1)S(1)} %gather_fusion.3), kind=kOutput, calls=%fused_computation.17 | convolution fusion | flops 9953280 | bytes 2222208 | tf_op jit(solution)/shard_map/while/body/eval_jaxpr/psjq,ptjq->pst/dot_general | solution.py:99
  76.7 4.0 %psum.15 = f32[32,9,9]{2,1,0:T(8,128)S(1)} all-reduce(f32[32,9,9]{2,1,0:T(8,128)S(1)} %fusion.13), channel_id=1, replica_groups=mesh['shift'=2,'space'=4,'orb'=2,'grid'=2] {'grid'}, use_global_device_ids=true, to_apply=%region_2.4 | all-reduce | flops 2592 | bytes 20736 | tf_op jit(solution)/shard_map/psum | solution.py:104
  80.8 0.8 copy.49
  (50 shorter events, 4.0 us)
Async XLA Ops:
  0.6 20.7 %copy-start.5 = (u32[32]{0:T(128)S(1)}, u32[32]{0:T(128)}, u32[]{:S(2)}) copy-start(u32[32]{0:T(128)} %constant.154) | copy-start | bytes 388
  0.6 20.6 %copy-start = (s32[8]{0:T(128)S(1)}, s32[8]{0:T(128)}, u32[]{:S(2)}) copy-start(s32[8]{0:T(128)} %param.10) | copy-start | bytes 100
  0.7 20.3 %copy-start.4 = (s32[32]{0:T(128)S(1)}, s32[32]{0:T(128)}, u32[]{:S(2)}) copy-start(s32[32]{0:T(128)} %param.14) | copy-start | bytes 388
  0.7 20.4 %copy-start.2 = (f32[32,9,9]{0,2,1:T(8,128)S(1)}, f32[32,9,9]{0,2,1:T(8,128)}, u32[]{:S(2)}) copy-start(f32[32,9,9]{0,2,1:T(8,128)} %param.11) | copy-start | bytes 31108
  0.7 22.1 %collective-permute-start = (s32[8]{0:T(128)}, s32[8]{0:T(128)S(1)}, u32[]{:S(2)}, u32[]{:S(2)}) collective-permute-start(s32[8]{0:T(128)} %param.10), channel_id=1, source_target_pairs={{0,4},{4,8},{8,12},{12,0},{1,5},{5,9},{9,13},{13,1},{2,6},{6,10},{... | collective-permute-start | bytes 104 | tf_op jit(solution)/shard_map/ppermute | solution.py:10
  3.8 19.3 %collective-permute-start.1 = (s32[8]{0:T(128)}, s32[8]{0:T(128)S(1)}, u32[]{:S(2)}, u32[]{:S(2)}) collective-permute-start(s32[8]{0:T(128)} %param.10), channel_id=1, source_target_pairs={{0,12},{4,0},{8,4},{12,8},{1,13},{5,1},{9,5},{13,9},{2,14},{6,2},{... | collective-permute-start | bytes 104 | tf_op jit(solution)/shard_map/ppermute | solution.py:10
  5.9 22.8 %collective-permute-start.2 = (bf16[8,9,15,128]{3,0,2,1:T(8,128)(2,1)}, bf16[8,9,15,128]{3,0,2,1:T(8,128)(2,1)S(1)}, u32[]{:S(2)}, u32[]{:S(2)}) collective-permute-start(bf16[8,9,15,128]{3,0,2,1:T(8,128)(2,1)} %param.9), channel_id=1, source_target_pairs={{0,4},{4,8},{8,12},{12,0},{1,5},{5,9},{9,13},{13,1},{2,6},{6,10},{... | collective-permute-start | bytes 829448 | tf_op jit(solution)/shard_map/ppermute | solution.py:10
  5.9 30.9 %collective-permute-start.3 = (bf16[8,9,15,128]{3,0,2,1:T(8,128)(2,1)}, bf16[8,9,15,128]{3,0,2,1:T(8,128)(2,1)S(1)}, u32[]{:S(2)}, u32[]{:S(2)}) collective-permute-start(bf16[8,9,15,128]{3,0,2,1:T(8,128)(2,1)} %param.9), channel_id=1, source_target_pairs={{0,12},{4,0},{8,4},{12,8},{1,13},{5,1},{9,5},{13,9},{2,14},{6,2},{... | collective-permute-start | bytes 829448 | tf_op jit(solution)/shard_map/ppermute | solution.py:10
  52.7 2.1 %copy-start.1 = (bf16[8,9,15,128]{3,0,2,1:T(8,128)(2,1)S(1)}, bf16[8,9,15,128]{3,0,2,1:T(8,128)(2,1)}, u32[]{:S(2)}) copy-start(bf16[8,9,15,128]{3,0,2,1:T(8,128)(2,1)} %param.9) | copy-start | bytes 829444
  54.7 15.6 %copy-start.3 = (f32[16,128]{1,0:T(8,128)S(1)}, f32[16,128]{1,0:T(8,128)}, u32[]{:S(2)}) copy-start(f32[16,128]{1,0:T(8,128)} %param.15) | copy-start | bytes 24580
  64.9 5.5 %collective-permute-start.4 = (f32[16,128]{1,0:T(8,128)S(1)}, f32[16,128]{1,0:T(8,128)S(1)}, u32[]{:S(2)}, u32[]{:S(2)}) collective-permute-start(f32[16,128]{1,0:T(8,128)S(1)} %slice.19), channel_id=1, source_target_pairs={{0,4},{4,8},{8,12},{12,0},{1,5},{5,9},{9,13},{13,1},{2,6},{6,10},{... | collective-permute-start | bytes 24584 | tf_op jit(solution)/shard_map/ppermute | solution.py:10
  71.0 3.7 %collective-permute-start.5 = (f32[16,128]{1,0:T(8,128)S(1)}, f32[16,128]{1,0:T(8,128)S(1)}, u32[]{:S(2)}, u32[]{:S(2)}) collective-permute-start(f32[16,128]{1,0:T(8,128)S(1)} %get-tuple-element.52), channel_id=1, source_target_pairs={{0,12},{4,0},{8,4},{12,8},{1,13},{5,1},{9,5},{13,9},{2,14},{6,2},{... | collective-permute-start | bytes 24584 | tf_op jit(solution)/shard_map/ppermute | solution.py:10
where the time goes:
time: 81.9 us; the launch traced here: 81.6 us
  blocking collectives  40.2 us (49%)
  local copies, waits for them, and re-layouts  13.5 us (16%)
  starting transfers between devices  9.06 us (11%)
  waiting for transfers between devices  9 us (11%)
  matrix products  5.04 us (6%)
  other arithmetic  3.28 us (4%)
  between operations  1.56 us (2%)
    ppermute x6, starting transfers between devices, shifted(): return lax.ppermute(value, axis, pairs)  9.06 us
    ppermute x6, waiting for transfers between devices, shifted(): return lax.ppermute(value, axis, pairs)  9 us
    all_gather x1, blocking collectives, on_device(): lax.all_gather(support, 'orb', axis=0, tiled=True)  8.41 us
    psum x1, blocking collectives, on_device(): summed = lax.psum(deposit, 'orb')  8.3 us
    all_gather x1, blocking collectives, on_device(): lax.all_gather(below_support, 'orb', axis=0, tiled=True)  7.96 us
    all_gather x1, blocking collectives, on_device(): lax.all_gather(above_support, 'orb', axis=0, tiled=True)  7.22 us
    gather x2, local copies, waits for them, and re-layouts, shift_planes(): jnp.take_along_axis(rows, jnp.clip(index, 0, box_depth - 1)[:, None, :, N...  5.32 us
    unnamed x1, blocking collectives  4.25 us
  transfers between devices with their start and end apart: 6, of which 2 were waited for; matrix products, arithmetic and copies ran while one was open for 7% of the time, Pallas kernels for 0%

commit v1 on v0

--- a/solution.py
+++ b/solution.py
@@ -83,7 +83,7 @@
         jnp.arange(2 * slab_rows, dtype=jnp.int32)[:, None, None] == local_plane[None, :, :]
     ).astype(jnp.float32)
     deposit = jnp.einsum("zaj,ajq->zq", placing, deposit_terms, precision=lax.Precision.HIGHEST)
-    summed = lax.psum(deposit, "orb")
+    summed = jnp.sum(lax.all_gather(deposit, "orb"), axis=0)
     incoming = shifted(summed[slab_rows:], "space", 1)
     density = summed[:slab_rows] + incoming
     potential = v_ext + respond(density)

time: 81.9 us -> 78 us (0.952)
  blocking collectives: 40.2 us -> 36.3 us
    psum x1 -> x0, blocking collectives: 8.3 us -> none  [on_device(): summed = lax.psum(deposit, 'orb')]
    all_gather x0 -> x1, blocking collectives: none -> 4.41 us  [on_device(): summed = jnp.sum(lax.all_gather(deposit, 'orb'), axis=0)]
where the time goes in v1:
time: 78 us; the launch traced here: 77.7 us
  blocking collectives  36.3 us (47%)
  local copies, waits for them, and re-layouts  13.5 us (17%)
  starting transfers between devices  9.07 us (12%)
  waiting for transfers between devices  9 us (12%)
  matrix products  5.05 us (6%)
  other arithmetic  3.29 us (4%)
  between operations  1.57 us (2%)
    ppermute x6, starting transfers between devices, shifted(): return lax.ppermute(value, axis, pairs)  9.07 us
    ppermute x6, waiting for transfers between devices, shifted(): return lax.ppermute(value, axis, pairs)  9 us
    all_gather x1, blocking collectives, on_device(): lax.all_gather(support, 'orb', axis=0, tiled=True)  8.41 us
    all_gather x1, blocking collectives, on_device(): lax.all_gather(below_support, 'orb', axis=0, tiled=True)  7.96 us
    all_gather x1, blocking collectives, on_device(): lax.all_gather(above_support, 'orb', axis=0, tiled=True)  7.22 us
    gather x2, local copies, waits for them, and re-layouts, shift_planes(): jnp.take_along_axis(rows, jnp.clip(index, 0, box_depth - 1)[:, None, :, N...  5.32 us
    all_gather x1, blocking collectives, on_device(): summed = jnp.sum(lax.all_gather(deposit, 'orb'), axis=0)  4.41 us
    unnamed x1, blocking collectives  4.25 us
  transfers between devices with their start and end apart: 6, of which 2 were waited for; matrix products, arithmetic and copies ran while one was open for 7% of the time, Pallas kernels for 0%

profile of v1, /device:TPU:0, one launch (start us, length us, event | category | flops | bytes accessed | tf_op | source)
XLA Modules:
  0.0 77.7 jit_solution(14169743790428218723)
XLA Ops:
  0.7 3.1 %collective-permute-start = (s32[8]{0:T(128)}, s32[8]{0:T(128)S(1)}, u32[]{:S(2)}, u32[]{:S(2)}) collective-permute-start(s32[8]{0:T(128)} %param.10), channel_id=1, source_target_pairs={{0,4},{4,8},{8,12},{12,0},{1,5},{5,9},{9,13},{13,1},{2,6},{6,10},{... | collective-permute-start | bytes 104 | tf_op jit(solution)/shard_map/ppermute | solution.py:10
  3.8 2.1 %collective-permute-start.1 = (s32[8]{0:T(128)}, s32[8]{0:T(128)S(1)}, u32[]{:S(2)}, u32[]{:S(2)}) collective-permute-start(s32[8]{0:T(128)} %param.10), channel_id=1, source_target_pairs={{0,12},{4,0},{8,4},{12,8},{1,13},{5,1},{9,5},{13,9},{2,14},{6,2},{... | collective-permute-start | bytes 104 | tf_op jit(solution)/shard_map/ppermute | solution.py:10
  5.9 3.8 %collective-permute-start.3 = (bf16[8,9,15,128]{3,0,2,1:T(8,128)(2,1)}, bf16[8,9,15,128]{3,0,2,1:T(8,128)(2,1)S(1)}, u32[]{:S(2)}, u32[]{:S(2)}) collective-permute-start(bf16[8,9,15,128]{3,0,2,1:T(8,128)(2,1)} %param.9), channel_id=1, source_target_pairs={{0,12},{4,0},{8,4},{12,8},{1,13},{5,1},{9,5},{13,9},{2,14},{6,2},{... | collective-permute-start | bytes 829448 | tf_op jit(solution)/shard_map/ppermute | solution.py:10
  9.7 8.4 %all_gather.28 = bf16[16,9,15,128]{3,0,2,1:T(8,128)(2,1)S(1)} all-gather(bf16[8,9,15,128]{3,0,2,1:T(8,128)(2,1)} %param.9), channel_id=1, replica_groups=mesh['shift'=2,'space'=4,'orb'=2,'grid'=2] {'orb'}, dimensions={0}, use_global_device_ids=true | all-gather | bytes 829440 | tf_op jit(solution)/shard_map/all_gather | solution.py:39
  18.1 0.7 compare_select_fusion.1
  18.8 0.7 compare_select_fusion.2
  19.5 1.4 %gather_fusion = s32[32]{0:T(128)S(1)} fusion(s32[8]{0:T(128)} %param.10, s32[1024]{0:T(1024)S(1)} %pad_clamp_fusion.1), kind=kCustom, calls=%fused_computation.1 | custom fusion | bytes 384 | tf_op jit(solution)/shard_map/gather | solution.py:52
  23.3 4.3 %all-reduce.3 = (s32[16]{0:T(128)S(1)}, s32[16]{0:T(128)S(1)}, s32[16]{0:T(128)S(1)}) all-reduce(s32[16]{0:T(128)S(1)} %dynamic-update-slice.2, s32[16]{0:T(128)S(1)} %dynamic-update-slice.1, s32[16]{0:T(128)S(1)} %dynamic-update-slice), channel_id=1, replica_groups=mesh['shift'=2,'space'=4,'orb'=2,'grid'=2] {'orb'}, use_global_device_ids=true, to_apply=%add.2 | all-reduce | flops 48 | bytes 384
  27.6 0.7 gather_fusion.1
  28.7 8.0 %all_gather.27 = bf16[16,9,15,128]{3,0,2,1:T(8,128)(2,1)S(1)} all-gather(bf16[8,9,15,128]{3,0,2,1:T(8,128)(2,1)S(1)} %collective-permute-done.2), channel_id=1, replica_groups=mesh['shift'=2,'space'=4,'orb'=2,'grid'=2] {'orb'}, dimensions={0}, use_global_device_ids=true | all-gather | bytes 829440 | tf_op jit(solution)/shard_map/all_gather | solution.py:38
  36.8 7.2 %all_gather.29 = bf16[16,9,15,128]{3,0,2,1:T(8,128)(2,1)S(1)} all-gather(bf16[8,9,15,128]{3,0,2,1:T(8,128)(2,1)S(1)} %collective-permute-done.3), channel_id=1, replica_groups=mesh['shift'=2,'space'=4,'orb'=2,'grid'=2] {'orb'}, dimensions={0}, use_global_device_ids=true | all-gather | bytes 829440 | tf_op jit(solution)/shard_map/all_gather | solution.py:40
  44.5 0.8 gather_fusion.2
  45.3 1.8 %copy.40 = bf16[32,9,15,128]{3,1,2,0:T(8,128)(2,1)} copy(bf16[32,9,15,128]{3,2,1,0:T(8,128)(2,1)S(1)} %gather_fusion.2) | data formatting | bytes 2211840 | tf_op jit(solution)/shard_map/while/body/eval_jaxpr/gather | solution.py:67
  47.1 5.2 %gather_fusion.4 = bf16[480,9,128]{2,1,0:T(8,128)(2,1)S(1)} fusion(bf16[32,9,15,128]{3,1,2,0:T(8,128)(2,1)} %copy.40, s32[480]{0:T(512)S(1)} %reshape.175), kind=kCustom, calls=%fused_computation.clone | custom fusion | bytes 2215680 | tf_op jit(solution)/shard_map/while/body/eval_jaxpr/jit(take_along_axis)/gather | solution.py:16
  52.7 2.1 %fusion.4 = f32[32,9,15,128]{3,1,2,0:T(8,128)S(1)} fusion(bf16[32,9,15,128]{3,2,0,1:T(8,128)(2,1)S(1)} %bitcast_select_fusion, f32[32,9,9]{2,1,0:T(8,128)S(1)} %copy.36, f32[32]{0:T(128)S(1)} %convert_element_type.16), kind=kOutput, calls=%fused_computation.9 | convolution fusion | flops 59722272 | bytes 3328256 | tf_op jit(solution)/shard_map/while/body/eval_jaxpr/pst,ptjq->psjq/dot_general | solution.py:68
  54.8 1.5 %fusion.10 = f32[8,15,128]{2,0,1:T(8,128)S(1)} fusion(f32[32,9,15,128]{3,1,2,0:T(8,128)S(1)} %fusion.4, bf16[8,9,15,128]{3,0,2,1:T(8,128)(2,1)S(1)} %copy-done.1, s32[32]{0:T(128)S(1)} %get-tuple-element.62), kind=kOutput, calls=%fused_computation.14 | convolution fusion | flops 53483776 | bytes 2549888 | tf_op jit(solution)/shard_map/while/body/eval_jaxpr/ap,psjq->asjq/dot_general | solution.py:73
  56.6 4.4 %all-gather = f32[64,128]{1,0:T(8,128)S(1)} all-gather(f32[32,128]{1,0:T(8,128)S(1)} %convolution_bitcast_fusion), channel_id=2, replica_groups=mesh['shift'=2,'space'=4,'orb'=2,'grid'=2] {'orb'}, dimensions={0}, use_global_device_ids=true | all-gather | bytes 49152 | tf_op jit(solution)/shard_map/all_gather | solution.py:86
  61.1 5.4 %collective-permute-done.4 = f32[16,128]{1,0:T(8,128)S(1)} collective-permute-done((f32[16,128]{1,0:T(8,128)S(1)}, f32[16,128]{1,0:T(8,128)S(1)}, u32[]{:S(2)}, u32[]{:S(2)}) %collective-permute-start.4) | collective-permute-done | bytes 8224 | tf_op jit(solution)/shard_map/ppermute | solution.py:10
  66.5 0.6 multiply_add_fusion
  67.2 3.6 %collective-permute-done.5 = f32[16,128]{1,0:T(8,128)S(1)} collective-permute-done((f32[16,128]{1,0:T(8,128)S(1)}, f32[16,128]{1,0:T(8,128)S(1)}, u32[]{:S(2)}, u32[]{:S(2)}) %collective-permute-start.5) | collective-permute-done | bytes 8224 | tf_op jit(solution)/shard_map/ppermute | solution.py:10
  71.1 0.8 %gather_fusion.3 = bf16[32,9,15,128]{3,2,1,0:T(8,128)(2,1)S(1)} fusion(bf16[8,9,15,128]{3,2,1,0:T(8,128)(2,1)S(1)} %copy.46, s32[1024]{0:T(1024)S(1)} %pad_clamp_fusion.1), kind=kCustom, calls=%fused_computation.4 | custom fusion | bytes 2211968 | tf_op jit(solution)/shard_map/while/body/eval_jaxpr/gather | solution.py:98
  71.9 1.0 %fusion.13 = f32[32,9,9]{2,1,0:T(8,128)S(1)} fusion(bf16[32,9,15,128]{3,2,0,1:T(8,128)(2,1)S(1)} %bitcast_select_fusion, bf16[32,9,15,128]{3,2,1,0:T(8,128)(2,1)S(1)} %gather_fusion.3), kind=kOutput, calls=%fused_computation.17 | convolution fusion | flops 9953280 | bytes 2222208 | tf_op jit(solution)/shard_map/while/body/eval_jaxpr/psjq,ptjq->pst/dot_general | solution.py:99
  72.8 4.0 %psum.7 = f32[32,9,9]{2,1,0:T(8,128)S(1)} all-reduce(f32[32,9,9]{2,1,0:T(8,128)S(1)} %fusion.13), channel_id=1, replica_groups=mesh['shift'=2,'space'=4,'orb'=2,'grid'=2] {'grid'}, use_global_device_ids=true, to_apply=%region_2.4 | all-reduce | flops 2592 | bytes 20736 | tf_op jit(solution)/shard_map/psum | solution.py:104
  77.0 0.8 copy.49
  (51 shorter events, 4.0 us)
Async XLA Ops:
  0.6 20.7 %copy-start.5 = (u32[32]{0:T(128)S(1)}, u32[32]{0:T(128)}, u32[]{:S(2)}) copy-start(u32[32]{0:T(128)} %constant.154) | copy-start | bytes 388
  0.6 20.6 %copy-start = (s32[8]{0:T(128)S(1)}, s32[8]{0:T(128)}, u32[]{:S(2)}) copy-start(s32[8]{0:T(128)} %param.10) | copy-start | bytes 100
  0.7 20.3 %copy-start.4 = (s32[32]{0:T(128)S(1)}, s32[32]{0:T(128)}, u32[]{:S(2)}) copy-start(s32[32]{0:T(128)} %param.14) | copy-start | bytes 388
  0.7 20.4 %copy-start.2 = (f32[32,9,9]{0,2,1:T(8,128)S(1)}, f32[32,9,9]{0,2,1:T(8,128)}, u32[]{:S(2)}) copy-start(f32[32,9,9]{0,2,1:T(8,128)} %param.11) | copy-start | bytes 31108
  0.7 22.1 %collective-permute-start = (s32[8]{0:T(128)}, s32[8]{0:T(128)S(1)}, u32[]{:S(2)}, u32[]{:S(2)}) collective-permute-start(s32[8]{0:T(128)} %param.10), channel_id=1, source_target_pairs={{0,4},{4,8},{8,12},{12,0},{1,5},{5,9},{9,13},{13,1},{2,6},{6,10},{... | collective-permute-start | bytes 104 | tf_op jit(solution)/shard_map/ppermute | solution.py:10
  3.8 19.3 %collective-permute-start.1 = (s32[8]{0:T(128)}, s32[8]{0:T(128)S(1)}, u32[]{:S(2)}, u32[]{:S(2)}) collective-permute-start(s32[8]{0:T(128)} %param.10), channel_id=1, source_target_pairs={{0,12},{4,0},{8,4},{12,8},{1,13},{5,1},{9,5},{13,9},{2,14},{6,2},{... | collective-permute-start | bytes 104 | tf_op jit(solution)/shard_map/ppermute | solution.py:10
  5.9 22.8 %collective-permute-start.2 = (bf16[8,9,15,128]{3,0,2,1:T(8,128)(2,1)}, bf16[8,9,15,128]{3,0,2,1:T(8,128)(2,1)S(1)}, u32[]{:S(2)}, u32[]{:S(2)}) collective-permute-start(bf16[8,9,15,128]{3,0,2,1:T(8,128)(2,1)} %param.9), channel_id=1, source_target_pairs={{0,4},{4,8},{8,12},{12,0},{1,5},{5,9},{9,13},{13,1},{2,6},{6,10},{... | collective-permute-start | bytes 829448 | tf_op jit(solution)/shard_map/ppermute | solution.py:10
  5.9 30.9 %collective-permute-start.3 = (bf16[8,9,15,128]{3,0,2,1:T(8,128)(2,1)}, bf16[8,9,15,128]{3,0,2,1:T(8,128)(2,1)S(1)}, u32[]{:S(2)}, u32[]{:S(2)}) collective-permute-start(bf16[8,9,15,128]{3,0,2,1:T(8,128)(2,1)} %param.9), channel_id=1, source_target_pairs={{0,12},{4,0},{8,4},{12,8},{1,13},{5,1},{9,5},{13,9},{2,14},{6,2},{... | collective-permute-start | bytes 829448 | tf_op jit(solution)/shard_map/ppermute | solution.py:10
  52.7 2.1 %copy-start.1 = (bf16[8,9,15,128]{3,0,2,1:T(8,128)(2,1)S(1)}, bf16[8,9,15,128]{3,0,2,1:T(8,128)(2,1)}, u32[]{:S(2)}) copy-start(bf16[8,9,15,128]{3,0,2,1:T(8,128)(2,1)} %param.9) | copy-start | bytes 829444
  54.7 11.8 %copy-start.3 = (f32[16,128]{1,0:T(8,128)S(1)}, f32[16,128]{1,0:T(8,128)}, u32[]{:S(2)}) copy-start(f32[16,128]{1,0:T(8,128)} %param.15) | copy-start | bytes 24580
  61.0 5.5 %collective-permute-start.4 = (f32[16,128]{1,0:T(8,128)S(1)}, f32[16,128]{1,0:T(8,128)S(1)}, u32[]{:S(2)}, u32[]{:S(2)}) collective-permute-start(f32[16,128]{1,0:T(8,128)S(1)} %slice.19), channel_id=1, source_target_pairs={{0,4},{4,8},{8,12},{12,0},{1,5},{5,9},{9,13},{13,1},{2,6},{6,10},{... | collective-permute-start | bytes 24584 | tf_op jit(solution)/shard_map/ppermute | solution.py:10
  67.1 3.7 %collective-permute-start.5 = (f32[16,128]{1,0:T(8,128)S(1)}, f32[16,128]{1,0:T(8,128)S(1)}, u32[]{:S(2)}, u32[]{:S(2)}) collective-permute-start(f32[16,128]{1,0:T(8,128)S(1)} %get-tuple-element.52), channel_id=1, source_target_pairs={{0,12},{4,0},{8,4},{12,8},{1,13},{5,1},{9,5},{13,9},{2,14},{6,2},{... | collective-permute-start | bytes 24584 | tf_op jit(solution)/shard_map/ppermute | solution.py:10
